TPU v7x, 512 devices: a whole 4x4x16 slice. The times are simulated.
512 devices in a mesh: row: 16 (over y_lo, x, core), col: 32 (over y_hi, z).
Axes of the slice: x: 4, y: 4 (y_hi: 2, y_lo: 2; y = y_hi * 2 + y_lo), z: 16, core: 2. Of those that a mesh axis runs over, the one named last changes fastest.
Arguments:
- amplitudes: float32 [8192, 256], P('row', 'col'), may hold values from -6 to 6
- integrals: float32 [256, 8192], P('row', 'col'), may hold values from -0.375 to 0.375
- occ_counts: int32 [8], replicated, may hold values from 1 to 10, 40 in all
- vir_counts: int32 [8], replicated, may hold values from 1 to 80, 400 in all
Outputs:
- symmetrized: float32 [8192, 8192], P('row', 'col')
Inputs may be any that keep to these rules, and one draw needn't show every extreme that they name: `occ_counts`: counts of occupied orbitals in the 8 irreducible representations, summing to 40. `vir_counts`: counts of virtual orbitals in the 8 irreducible representations, summing to 400.
All inputs are finite; a program needn't handle non-finite values.
Results may differ from a plain program's by a relative error of at most 0.00007.
Values sent between devices are 32-bit elements; how exact they have to be, the bound alone decides.
A program may use at most 64 MiB of HBM per device.

v0:
```python
import jax
import jax.numpy as jnp
from jax import lax
from jax.sharding import PartitionSpec as P

NVIR = 400


def orbital_irreps(orbitals, counts):
    bounds = jnp.cumsum(counts)[:-1]
    return jnp.sum((orbitals[:, None] >= bounds[None, :]).astype(jnp.int32), axis=1)


def pair_labels(positions, occ_counts, vir_counts):
    occ_part = orbital_irreps(positions // NVIR, occ_counts)
    vir_part = orbital_irreps(positions % NVIR, vir_counts)
    return jnp.bitwise_xor(occ_part, vir_part)


def exact_dot(left, right):
    return jnp.dot(left, right, precision=lax.Precision.HIGHEST, preferred_element_type=jnp.float32)


def assemble(received, row_count, narrow):
    grouped = received.reshape(row_count, 2, -1).transpose(1, 0, 2).reshape(2, narrow, narrow)
    return grouped.transpose(1, 0, 2).reshape(narrow, 2 * narrow).T


def per_device(amplitudes, integrals, occ_counts, vir_counts):
    row_count = lax.axis_size("row")
    col_count = lax.axis_size("col")
    row_index = lax.axis_index("row")
    col_index = lax.axis_index("col")
    tall = amplitudes.shape[0]
    narrow = integrals.shape[1]
    row_labels = pair_labels(
        row_index * tall + jnp.arange(tall, dtype=jnp.int32), occ_counts, vir_counts
    )
    col_labels = pair_labels(
        col_index * narrow + jnp.arange(narrow, dtype=jnp.int32), occ_counts, vir_counts
    )
    allowed = row_labels[:, None] == col_labels[None, :]
    parity = col_index % 2
    int_cols = lax.all_gather(integrals, "row", axis=0, tiled=True)
    product = exact_dot(lax.all_gather(amplitudes, "col", axis=1, tiled=True), int_cols)
    flattened = product.reshape(2, row_count, -1)
    oriented = jnp.where(parity == 0, flattened, flattened[::-1])
    outgoing = oriented.transpose(1, 0, 2).reshape(col_count, -1)
    section_one = lax.all_to_all(outgoing, "col", split_axis=0, concat_axis=0, tiled=True)
    section_two = lax.all_to_all(section_one, "row", split_axis=0, concat_axis=0, tiled=True)
    paired = section_two.reshape(row_count, 2, -1)
    paired = jnp.where(parity == 0, paired, paired[:, ::-1]).reshape(col_count, -1)
    section_three = lax.all_to_all(paired, "col", split_axis=0, concat_axis=0, tiled=True)
    arrived = section_three.reshape(row_count, 2, -1)
    arrived = jnp.where(parity == 0, arrived, arrived[:, ::-1]).reshape(col_count, -1)
    mirrored = assemble(arrived, row_count, narrow)
    return jnp.where(allowed, product + mirrored, 0.0)


def solution(mesh):
    placed = (P("row", "col"), P("row", "col"), P(), P())
    return jax.shard_map(
        per_device, mesh=mesh, in_specs=placed, out_specs=P("row", "col"), check_vma=False
    )
```

profile of v0, /device:TPU:32, one launch (start us, length us, event | category | flops | bytes accessed | tf_op | source)
XLA Modules:
  0.0 209.4 jit_solution(9081670944879843364)
XLA Ops:
  0.0 0.7 copy-done
  0.7 81.1 %all_gather.6 = f32[512,256]{0,1:T(8,128)S(1)} all-gather(f32[512,8]{0,1:T(8,128)S(1)} %copy-done), channel_id=1, replica_groups=mesh['row'=16,'col'=32] {'col'}, dimensions={1}, use_global_device_ids=true | all-gather | bytes 540672 | tf_op jit(solution)/shard_map/all_gather | solution.py:45
  81.8 19.5 %all_gather.7 = f32[256,256]{1,0:T(8,128)S(1)} all-gather(f32[16,256]{1,0:T(8,128)S(1)} %copy-done.1), channel_id=1, replica_groups=mesh['row'=16,'col'=32] {'row'}, dimensions={0}, use_global_device_ids=true | all-gather | bytes 278528 | tf_op jit(solution)/shard_map/all_gather | solution.py:44
  101.3 1.0 fusion.8
  102.3 0.1 reshape.88
  102.4 0.4 copy.20
  102.8 1.9 rev.9
  104.7 0.5 select_bitcast_fusion.1
  105.3 0.8 all_to_all.24
  106.1 41.9 %all_to_all.29 = f32[32,1,4096]{2,1,0:T(1,128)S(1)} all-to-all(f32[32,1,4096]{2,1,0:T(1,128)S(1)} %all_to_all.24), channel_id=1, replica_groups=mesh['row'=16,'col'=32] {'col'}, dimensions={0} | all-to-all | bytes 1048576 | tf_op jit(solution)/shard_map/all_to_all | solution.py:49
  147.9 1.2 reduce
  149.2 0.3 all_to_all.20
  149.5 13.5 %all_to_all.30 = f32[16,2,4096]{2,1,0:T(2,128)S(1)} all-to-all(f32[16,2,4096]{2,1,0:T(2,128)S(1)} %all_to_all.20), channel_id=1, replica_groups=mesh['row'=16,'col'=32] {'row'}, dimensions={0} | all-to-all | bytes 1048576 | tf_op jit(solution)/shard_map/all_to_all | solution.py:50
  163.0 1.9 rev.10
  164.9 1.6 all_to_all.25
  166.5 4.5 %all-to-all-start.2 = ((f32[32,1,4096]{2,1,0:T(1,128)}), f32[32,1,4096]{2,1,0:T(1,128)S(1)}, u32[]{:S(2)}, u32[]{:S(2)}) async-start(f32[32,1,4096]{2,1,0:T(1,128)} %all_to_all.25), calls=%async_computation.2 | async-start | bytes 1048576 | tf_op jit(solution)/shard_map/all_to_all | solution.py:53
  171.1 0.6 copy-done.2
  171.8 0.2 reduce-window.9
  171.9 0.7 copy-done.3
  172.6 0.2 reduce-window.6
  172.8 0.1 convert_reduce_fusion.2
  172.9 0.1 convert_reduce_fusion.3
  173.0 0.1 convert_reduce_fusion
  173.1 0.1 convert_reduce_fusion.1
  173.2 30.9 %all-to-all-done.2 = f32[32,1,4096]{2,1,0:T(1,128)S(1)} async-done(((f32[32,1,4096]{2,1,0:T(1,128)}), f32[32,1,4096]{2,1,0:T(1,128)S(1)}, u32[]{:S(2)}, u32[]{:S(2)}) %all-to-all-start.2) | async-done | bytes 524320 | tf_op jit(solution)/shard_map/all_to_all | solution.py:53
  204.1 1.2 reduce.1
  205.3 0.3 reshape.89
  205.6 1.9 rev.11
  207.5 0.3 select_bitcast_fusion
  207.8 0.3 copy.23
  208.3 0.2 copy.24
  208.5 0.9 fusion
  (13 shorter events, 0.2 us)
Async XLA Ops:
  0.0 0.7 copy-start
  0.7 81.1 %copy-start.1 = (f32[16,256]{1,0:T(8,128)S(1)}, f32[16,256]{1,0:T(8,128)}, u32[]{:S(2)}) copy-start(f32[16,256]{1,0:T(8,128)} %param.5) | copy-start | bytes 49156
  166.5 37.5 %all-to-all-start.2 = ((f32[32,1,4096]{2,1,0:T(1,128)}), f32[32,1,4096]{2,1,0:T(1,128)S(1)}, u32[]{:S(2)}, u32[]{:S(2)}) async-start(f32[32,1,4096]{2,1,0:T(1,128)} %all_to_all.25), calls=%async_computation.2 | async-start | bytes 1048576 | tf_op jit(solution)/shard_map/all_to_all | solution.py:53
  171.1 0.7 copy-start.2
  171.9 0.7 copy-start.3
where the time goes:
time: 210 us; the launch traced here: 209 us
  blocking collectives  156 us (74%)
  waiting for transfers between devices  30.9 us (15%)
  local copies, waits for them, and re-layouts  11.9 us (6%)
  other arithmetic  5.09 us (2%)
  starting transfers between devices  4.54 us (2%)
    all_gather x1, blocking collectives, per_device(): lax.all_gather(amplitudes, 'col', axis=1, tiled=True)  81.1 us
    all_to_all x1, blocking collectives, per_device(): lax.all_to_all(outgoing, 'col', split_axis=0, concat_axis=0, tiled=True)  41.9 us
    all_to_all x1, waiting for transfers between devices, per_device(): lax.all_to_all(paired, 'col', split_axis=0, concat_axis=0, tiled=True)  30.9 us
    all_gather x1, blocking collectives, per_device(): int_cols = lax.all_gather(integrals, 'row', axis=0, tiled=True)  19.5 us
    all_to_all x1, blocking collectives, per_device(): lax.all_to_all(section_one, 'row', split_axis=0, concat_axis=0, tiled=True)  13.5 us
    all_to_all x1, starting transfers between devices, per_device(): lax.all_to_all(paired, 'col', split_axis=0, concat_axis=0, tiled=True)  4.54 us
  transfers between devices with their start and end apart: 1, of which 1 were waited for; matrix products, arithmetic and copies ran while one was open for 0% of the time, Pallas kernels for 0%

commit v1 on v0

--- a/solution.py
+++ b/solution.py
@@ -41,7 +41,9 @@
     )
     allowed = row_labels[:, None] == col_labels[None, :]
     parity = col_index % 2
-    int_cols = lax.all_gather(integrals, "row", axis=0, tiled=True)
+    int_cols = jnp.concatenate(
+        lax.all_to_all(jnp.stack([integrals] * lax.axis_size("row")), "row", 0, 0), axis=0
+    )
     product = exact_dot(lax.all_gather(amplitudes, "col", axis=1, tiled=True), int_cols)
     flattened = product.reshape(2, row_count, -1)
     oriented = jnp.where(parity == 0, flattened, flattened[::-1])

time: 210 us -> 190 us (0.905)
  blocking collectives: 156 us -> 129 us
  starting transfers between devices: 4.54 us -> 10.2 us
    all_gather x1 -> x0, blocking collectives: 19.5 us -> none  [per_device(): int_cols = lax.all_gather(integrals, 'row', axis=0, tiled=True)]
    all_to_all x1, blocking collectives: 41.9 us -> 30.8 us  [per_device(): lax.all_to_all(outgoing, 'col', split_axis=0, concat_axis=0, tiled=True)]
    all_to_all x0 -> x1, starting transfers between devices: none -> 5.42 us  [per_device(): lax.all_to_all(jnp.stack([integrals] * lax.axis_size('row')), 'row', 0, 0)]
    all_to_all x1, blocking collectives: 13.5 us -> 17.6 us  [per_device(): lax.all_to_all(section_one, 'row', split_axis=0, concat_axis=0, tiled=True)]
  transfers between devices with their start and end apart: 1 -> 2, of which waited for: 1 -> 1; matrix products, arithmetic and copies ran while one was open for 0% -> 0% of each run, Pallas kernels for 0% -> 0%
where the time goes in v1:
time: 190 us
  blocking collectives  129 us (68%)
  waiting for transfers between devices  30.9 us (16%)
  local copies, waits for them, and re-layouts  13.3 us (7%)
  starting transfers between devices  10.2 us (5%)
  other arithmetic  5.09 us (3%)
    all_gather x1, blocking collectives, per_device(): lax.all_gather(amplitudes, 'col', axis=1, tiled=True)  80.6 us
    all_to_all x1, waiting for transfers between devices, per_device(): lax.all_to_all(paired, 'col', split_axis=0, concat_axis=0, tiled=True)  30.9 us
    all_to_all x1, blocking collectives, per_device(): lax.all_to_all(outgoing, 'col', split_axis=0, concat_axis=0, tiled=True)  30.8 us
    all_to_all x1, blocking collectives, per_device(): lax.all_to_all(section_one, 'row', split_axis=0, concat_axis=0, tiled=True)  17.6 us
    all_to_all x1, starting transfers between devices, per_device(): lax.all_to_all(jnp.stack([integrals] * lax.axis_size('row')), 'row', 0, 0)  5.42 us
    all_to_all x1, starting transfers between devices, per_device(): lax.all_to_all(paired, 'col', split_axis=0, concat_axis=0, tiled=True)  4.73 us
  transfers between devices with their start and end apart: 2, of which 1 were waited for; matrix products, arithmetic and copies ran while one was open for 0% of the time, Pallas kernels for 0%

profile of v1, /device:TPU:32, one launch (start us, length us, event | category | flops | bytes accessed | tf_op | source)
XLA Modules:
  0.0 189.6 jit_solution(1494604112932603913)
XLA Ops:
  0.0 1.4 stack.2
  1.4 5.4 %all-to-all-start = ((f32[16,16,256]{2,1,0:T(8,128)}), f32[16,16,256]{2,1,0:T(8,128)S(1)}, u32[]{:S(2)}, u32[]{:S(2)}) async-start(f32[16,16,256]{2,1,0:T(8,128)} %stack.2), calls=%async_computation | async-start | bytes 524288 | tf_op jit(solution)/shard_map/all_to_all | solution.py:45
  6.9 0.7 copy-done
  7.6 80.6 %all_gather.3 = f32[512,256]{0,1:T(8,128)S(1)} all-gather(f32[512,8]{0,1:T(8,128)S(1)} %copy-done), channel_id=1, replica_groups=mesh['row'=16,'col'=32] {'col'}, dimensions={1}, use_global_device_ids=true | all-gather | bytes 540672 | tf_op jit(solution)/shard_map/all_gather | solution.py:47
  88.2 1.0 fusion.8
  89.2 0.1 reshape.94
  89.3 0.4 copy.20
  89.8 1.9 %rev.9 = f32[2,16,4096]{2,0,1:T(2,128)S(1)} reverse(f32[2,16,4096]{2,0,1:T(2,128)S(1)} %copy.20), dimensions={0} | reverse | bytes 1048576 | tf_op jit(solution)/shard_map/rev | solution.py:49
  91.7 0.5 select_bitcast_fusion.1
  92.2 0.8 all_to_all.28
  93.0 30.8 %all_to_all.34 = f32[32,1,4096]{2,1,0:T(1,128)S(1)} all-to-all(f32[32,1,4096]{2,1,0:T(1,128)S(1)} %all_to_all.28), channel_id=1, replica_groups=mesh['row'=16,'col'=32] {'col'}, dimensions={0} | all-to-all | bytes 1048576 | tf_op jit(solution)/shard_map/all_to_all | solution.py:51
  123.8 1.2 reduce
  125.1 0.3 all_to_all.24
  125.4 17.6 %all_to_all.35 = f32[16,2,4096]{2,1,0:T(2,128)S(1)} all-to-all(f32[16,2,4096]{2,1,0:T(2,128)S(1)} %all_to_all.24), channel_id=1, replica_groups=mesh['row'=16,'col'=32] {'row'}, dimensions={0} | all-to-all | bytes 1048576 | tf_op jit(solution)/shard_map/all_to_all | solution.py:52
  143.0 1.9 rev.10
  145.0 1.6 all_to_all.29
  146.6 4.7 %all-to-all-start.3 = ((f32[32,1,4096]{2,1,0:T(1,128)}), f32[32,1,4096]{2,1,0:T(1,128)S(1)}, u32[]{:S(2)}, u32[]{:S(2)}) async-start(f32[32,1,4096]{2,1,0:T(1,128)} %all_to_all.29), calls=%async_computation.3 | async-start | bytes 1048576 | tf_op jit(solution)/shard_map/all_to_all | solution.py:55
  151.3 0.6 copy-done.1
  152.0 0.2 reduce-window.9
  152.1 0.7 copy-done.2
  152.8 0.2 reduce-window.6
  153.0 0.1 convert_reduce_fusion.2
  153.1 0.1 convert_reduce_fusion.3
  153.2 0.1 convert_reduce_fusion
  153.4 30.9 %all-to-all-done.3 = f32[32,1,4096]{2,1,0:T(1,128)S(1)} async-done(((f32[32,1,4096]{2,1,0:T(1,128)}), f32[32,1,4096]{2,1,0:T(1,128)S(1)}, u32[]{:S(2)}, u32[]{:S(2)}) %all-to-all-start.3) | async-done | bytes 524320 | tf_op jit(solution)/shard_map/all_to_all | solution.py:55
  184.3 1.2 reduce.1
  185.5 0.3 reshape.95
  185.8 1.9 %rev.11 = f32[16,2,4096]{2,1,0:T(2,128)S(1)} reverse(f32[16,2,4096]{2,1,0:T(2,128)S(1)} %reshape.95), dimensions={1} | reverse | bytes 1048576 | tf_op jit(solution)/shard_map/rev | solution.py:57
  187.7 0.3 select_bitcast_fusion
  188.1 0.3 copy.23
  188.5 0.2 copy.24
  188.7 0.9 fusion
  (13 shorter events, 0.3 us)
Async XLA Ops:
  1.4 86.8 %all-to-all-start = ((f32[16,16,256]{2,1,0:T(8,128)}), f32[16,16,256]{2,1,0:T(8,128)S(1)}, u32[]{:S(2)}, u32[]{:S(2)}) async-start(f32[16,16,256]{2,1,0:T(8,128)} %stack.2), calls=%async_computation | async-start | bytes 524288 | tf_op jit(solution)/shard_map/all_to_all | solution.py:45
  6.9 0.7 copy-start
  146.6 37.7 %all-to-all-start.3 = ((f32[32,1,4096]{2,1,0:T(1,128)}), f32[32,1,4096]{2,1,0:T(1,128)S(1)}, u32[]{:S(2)}, u32[]{:S(2)}) async-start(f32[32,1,4096]{2,1,0:T(1,128)} %all_to_all.29), calls=%async_computation.3 | async-start | bytes 1048576 | tf_op jit(solution)/shard_map/all_to_all | solution.py:55
  151.3 0.7 copy-start.1
  152.1 0.7 copy-start.2
